TPU v7x, 512 devices: a whole 4x8x8 slice. The times are simulated.
512 devices in a mesh: leaf: 32 (over x, y), front: 16 (over z, core).
Axes of the slice: x: 4, y: 8, z: 8, core: 2. Of those that a mesh axis runs over, the one named last changes fastest.
Arguments:
- child_pivot: float32 [32, 512, 512], P('leaf', 'front')
- child_panel: float32 [32, 2048, 512], P('leaf', 'front'), may hold values from -0.9 to 0.9
- anc_front: float32 [32, 16, 512, 512], P('leaf', 'front')
- dest_list: int32 [32, 16], replicated, may hold values from 0 to 31, as said below
- col_list: int32 [32, 16], replicated, may hold values from 0 to 3, as said below
- row_list: int32 [32, 16], replicated, may hold values from 0 to 3, as said below
Outputs:
- child_lower: float32 [32, 512, 512], P('leaf', 'front')
- child_factor: float32 [32, 2048, 512], P('leaf', 'front')
- anc_factor: float32 [32, 16, 512, 512], P('leaf', 'front')
Inputs may be any that keep to these rules, and one draw needn't show every extreme that they name: dest_list[g, j] is g with exactly one bit of its index flipped; every group that row g names is named there by exactly 4 column blocks, so row g names 4 different groups. `col_list`: column blocks of one group that name the same group in dest_list have different entries here. row_list[g, f] is 1 or more for f < 4.
All inputs are finite; a program needn't handle non-finite values.
Results may differ from a plain program's by a relative error of at most 0.0001.
Values sent between devices are 32-bit elements; how exact they have to be, the bound alone decides.
No kernel may reach another device: no remote copies, remote signals or barrier semaphores. Data moves between devices by JAX's collectives and lax.ppermute only.
A program may use at most 64 MiB of HBM per device.

v0:
```python
import jax
import jax.numpy as jnp
from jax import lax
from jax.sharding import PartitionSpec as P


def swapped(value, axis, distance):
    mask = 2**distance
    pairs = [(source, source ^ mask) for source in range(lax.axis_size(axis))]
    return lax.ppermute(value, axis, pairs)


def schur_block(left, right):
    return lax.dot_general(
        left,
        right,
        (((1,), (1,)), ((), ())),
        precision=lax.Precision.HIGHEST,
        preferred_element_type=jnp.float32,
    )


def slot_ranks(dest_list):
    count = dest_list.shape[1]
    positions = jnp.arange(count, dtype=jnp.int32)
    earlier = positions[:, None] > positions[None, :]
    same = dest_list[:, :, None] == dest_list[:, None, :]
    return jnp.sum((same & earlier[None]).astype(jnp.int32), axis=2)


def lookup_rows(table, sender_ids):
    leaf_ids = jnp.arange(table.shape[0], dtype=jnp.int32)
    hits = (sender_ids[:, None] == leaf_ids[None, :]).astype(jnp.int32)
    return jnp.sum(hits[:, :, None] * table[None], axis=1)


def pick_blocks(own_targets, own_ranks, target, slot_ids, update_blocks):
    select = ((own_targets[None, :] == target) & (own_ranks[None, :] == slot_ids[:, None])).astype(
        jnp.float32
    )
    return jnp.einsum("kj,xjy->kxy", select, update_blocks, precision=lax.Precision.HIGHEST)


def per_device(child_pivot, child_panel, anc_front, dest_list, col_list, row_list):
    front_count = lax.axis_size("front")
    front_pos = lax.axis_index("front")
    group = lax.axis_index("leaf")
    slab = child_pivot.shape[1]
    block = child_panel.shape[1]
    width = child_panel.shape[2]
    blocks_wide = width // block
    row_slots = anc_front.shape[2] // block
    pivot = lax.all_gather(child_pivot[0], "front", axis=0, tiled=True)
    lower = jnp.linalg.cholesky(pivot)
    lower_rows = lax.dynamic_slice_in_dim(lower, front_pos * slab, slab, 0)
    panel = lax.linalg.triangular_solve(
        lower, child_panel[0], left_side=False, lower=True, transpose_a=True
    )
    update = schur_block(panel, lax.all_gather(panel, "front", axis=0, tiled=True))
    ranks = slot_ranks(dest_list)
    slot_ids = jnp.arange(blocks_wide, dtype=jnp.int32)
    own_targets = lax.dynamic_index_in_dim(dest_list, group, 0, keepdims=False)
    own_ranks = lax.dynamic_index_in_dim(ranks, group, 0, keepdims=False)
    update_blocks = update.reshape(block, front_count, block)
    levels = lax.axis_size("leaf").bit_length() - 1
    arrived = []
    partners = []
    for level_bit in range(levels):
        partner = jnp.bitwise_xor(group, 1 << level_bit)
        outgoing = pick_blocks(own_targets, own_ranks, partner, slot_ids, update_blocks)
        arrived.append(swapped(outgoing, "leaf", level_bit))
        partners.append(partner)
    received = jnp.stack(arrived)
    sender_ids = jnp.stack(partners)
    src_dest = lookup_rows(dest_list, sender_ids)
    src_ranks = lookup_rows(ranks, sender_ids)
    src_cols = lookup_rows(col_list, sender_ids)
    src_rows = lookup_rows(row_list, sender_ids)
    match = (src_dest == group)[:, None, :] & (src_ranks[:, None, :] == slot_ids[None, :, None])
    live = jnp.sum(match.astype(jnp.int32), axis=2)
    column_of = jnp.sum(jnp.where(match, src_cols[:, None, :], 0), axis=2)
    row_of = lax.dynamic_index_in_dim(src_rows, front_pos, 1, keepdims=False)
    slot_rows = jnp.arange(row_slots, dtype=jnp.int32)
    slot_cols = jnp.arange(blocks_wide, dtype=jnp.int32)
    weight = (
        (live[:, :, None, None] == 1)
        & (row_of[:, None, None, None] == slot_rows[None, None, :, None])
        & (column_of[:, :, None, None] == slot_cols[None, None, None, :])
    ).astype(jnp.float32)
    incoming = jnp.einsum("gkrc,gkxy->rxcy", weight, received, precision=lax.Precision.HIGHEST)
    assembled = anc_front[0, 0] - incoming.reshape(row_slots * block, width)
    owner = front_pos < blocks_wide
    owner_pos = jnp.minimum(front_pos, blocks_wide - 1)
    top_rows = jnp.where(owner, assembled[:block], 0.0)
    contribution = lax.dynamic_update_slice_in_dim(
        jnp.zeros((width, width), jnp.float32), top_rows, owner_pos * block, 0
    )
    anc_pivot = lax.psum(contribution, "front")
    anc_lower = jnp.linalg.cholesky(anc_pivot)
    solved = lax.linalg.triangular_solve(
        anc_lower, assembled, left_side=False, lower=True, transpose_a=True
    )
    own_lower = lax.dynamic_slice_in_dim(anc_lower, owner_pos * block, block, 0)
    padded = lax.dynamic_update_slice_in_dim(jnp.zeros_like(solved), own_lower, 0, 0)
    row_ids = jnp.arange(row_slots * block, dtype=jnp.int32)
    mask = (row_ids < block)[:, None] & owner
    anc_out = jnp.where(mask, padded, solved)
    return (lower_rows[None], panel[None], anc_out[None, None])


def solution(mesh):
    in_specs = (
        P("leaf", "front", None),
        P("leaf", "front", None),
        P("leaf", "front", None, None),
        P(),
        P(),
        P(),
    )
    out_specs = (P("leaf", "front", None), P("leaf", "front", None), P("leaf", "front", None, None))
    return jax.shard_map(
        per_device, mesh=mesh, in_specs=in_specs, out_specs=out_specs, check_vma=False
    )
```

profile of v0, /device:TPU:1, one launch (start us, length us, event | category | flops | bytes accessed | tf_op | source)
XLA Modules:
  0.0 557.9 jit_solution(7262948002128751580)
XLA Ops:
  8.8 49.6 %all-gather.6.cloned.1.call-done = f32[1,512,512]{2,0,1:T(1,128)} async-done(((f32[1,32,512]{2,0,1:T(1,128)}), f32[1,512,512]{2,0,1:T(1,128)}) %all-gather.6.cloned.1.call-update) | async-done | bytes 1048592 | tf_op jit(solution)/shard_map/all_gather | solution.py:53
  61.2 11.7 %cholesky.286 = f32[128,128]{1,0:T(8,128)S(1)} custom-call(f32[128,128]{1,0:T(8,128)S(1)} %cholesky.426), custom_call_target="Cholesky" | custom-call | tf_op jit(solution)/shard_map/jit(cholesky)/cholesky | solution.py:54
  73.0 9.8 %custom-call.31 = f32[1,128,128]{1,2,0:T(8,128)S(1)} custom-call(f32[1,128,128]{2,1,0:T(8,128)S(1)} %get-tuple-element.123), custom_call_target="InvertDiagBlocksLowerTriangular" | custom-call | tf_op jit(solution)/shard_map/jit(cholesky)/cholesky | solution.py:54
  83.6 11.7 %cholesky.305 = f32[128,128]{1,0:T(8,128)S(1)} custom-call(f32[128,128]{1,0:T(8,128)S(1)} %cholesky.430), custom_call_target="Cholesky" | custom-call | tf_op jit(solution)/shard_map/jit(cholesky)/cholesky | solution.py:54
  95.5 10.0 %custom-call.32 = f32[1,128,128]{1,2,0:T(8,128)S(1)} custom-call(f32[1,128,128]{2,1,0:T(8,128)S(1)} %get-tuple-element.121), custom_call_target="InvertDiagBlocksLowerTriangular" | custom-call | tf_op jit(solution)/shard_map/jit(cholesky)/cholesky | solution.py:54
  106.6 11.7 %cholesky.326 = f32[128,128]{1,0:T(8,128)S(1)} custom-call(f32[128,128]{1,0:T(8,128)S(1)} %cholesky.435), custom_call_target="Cholesky" | custom-call | tf_op jit(solution)/shard_map/jit(cholesky)/cholesky | solution.py:54
  118.4 9.8 %custom-call.33 = f32[1,128,128]{1,2,0:T(8,128)S(1)} custom-call(f32[1,128,128]{2,1,0:T(8,128)S(1)} %get-tuple-element.119), custom_call_target="InvertDiagBlocksLowerTriangular" | custom-call | tf_op jit(solution)/shard_map/jit(cholesky)/cholesky | solution.py:54
  129.1 12.1 %cholesky.343 = f32[128,128]{1,0:T(8,128)S(1)} custom-call(f32[128,128]{1,0:T(8,128)S(1)} %convolution_subtract_fusion.11), custom_call_target="Cholesky" | custom-call | tf_op jit(solution)/shard_map/jit(cholesky)/cholesky | solution.py:54
  147.2 8.5 %while.2 = (s32[]{:T(128)}, f32[512,512]{0,1:T(8,128)S(1)}, s32[4,2]{0,1:T(2,128)S(1)}, f32[4,128,128]{2,1,0:T(8,128)S(1)}, s32[]{:T(128)}) while((s32[]{:T(128)}, f32[512,512]{0,1:T(8,128)S(1)}, s32[4,2]{0,1:T(2,128)S(1)}, f32[4,128,128]{2,1,0:T(8,128)S(1)}, s32[]{:T(128)}) %tuple.71), condition=%wide.while_cond, body=%wide.while_body.sunk | while | flops 2 | bytes 393329 | solution.py:56
  155.6 39.3 %custom-call.26 = f32[4,128,128]{1,2,0:T(8,128)S(1)} custom-call(f32[4,128,128]{2,1,0:T(8,128)S(1)} %get-tuple-element.11), custom_call_target="InvertDiagBlocksLowerTriangular" | custom-call | tf_op jit(solution)/shard_map/triangular_solve | solution.py:56
  201.5 47.6 %all-gather.4.cloned.1.call-done = f32[2048,512]{0,1:T(8,128)} async-done(((f32[128,512]{0,1:T(8,128)}), f32[2048,512]{0,1:T(8,128)}) %all-gather.4.cloned.1.call-update) | async-done | bytes 4194320 | tf_op jit(solution)/shard_map/all_gather | solution.py:59
  249.1 4.5 convolution_bitcast_fusion
  270.3 4.5 collective-permute-start.4
  274.9 9.5 %collective-permute-done.1 = f32[4,128,128]{2,0,1:T(4,128)S(1)} collective-permute-done((f32[4,128,128]{2,0,1:T(4,128)S(1)}, f32[4,128,128]{2,0,1:T(4,128)S(1)}, u32[]{:S(2)}, u32[]{:S(2)}) %collective-permute-start.1) | collective-permute-done | bytes 262176 | tf_op jit(solution)/shard_map/ppermute | solution.py:10
  290.5 113.9 %all-reduce.4.cloned.1.call-done = f32[512,512]{0,1:T(8,128)} async-done(((f32[512,512]{0,1:T(8,128)}), f32[512,512]{0,1:T(8,128)}) %all-reduce.4.cloned.1.call-update) | async-done | bytes 1048592 | tf_op jit(solution)/shard_map/psum | solution.py:98
  407.3 11.7 %cholesky.358 = f32[128,128]{1,0:T(8,128)S(1)} custom-call(f32[128,128]{1,0:T(8,128)S(1)} %cholesky.439), custom_call_target="Cholesky" | custom-call | tf_op jit(solution)/shard_map/jit(cholesky)/cholesky | solution.py:99
  419.1 9.8 %custom-call.34 = f32[1,128,128]{1,2,0:T(8,128)S(1)} custom-call(f32[1,128,128]{2,1,0:T(8,128)S(1)} %get-tuple-element.117), custom_call_target="InvertDiagBlocksLowerTriangular" | custom-call | tf_op jit(solution)/shard_map/jit(cholesky)/cholesky | solution.py:99
  431.6 11.9 %cholesky.377 = f32[128,128]{1,0:T(8,128)S(1)} custom-call(f32[128,128]{1,0:T(8,128)S(1)} %cholesky.443), custom_call_target="Cholesky" | custom-call | tf_op jit(solution)/shard_map/jit(cholesky)/cholesky | solution.py:99
  443.6 9.8 %custom-call.35 = f32[1,128,128]{1,2,0:T(8,128)S(1)} custom-call(f32[1,128,128]{2,1,0:T(8,128)S(1)} %get-tuple-element.115), custom_call_target="InvertDiagBlocksLowerTriangular" | custom-call | tf_op jit(solution)/shard_map/jit(cholesky)/cholesky | solution.py:99
  455.4 11.7 %cholesky.398 = f32[128,128]{1,0:T(8,128)S(1)} custom-call(f32[128,128]{1,0:T(8,128)S(1)} %cholesky.448), custom_call_target="Cholesky" | custom-call | tf_op jit(solution)/shard_map/jit(cholesky)/cholesky | solution.py:99
  467.3 9.8 %custom-call.36 = f32[1,128,128]{1,2,0:T(8,128)S(1)} custom-call(f32[1,128,128]{2,1,0:T(8,128)S(1)} %get-tuple-element.113), custom_call_target="InvertDiagBlocksLowerTriangular" | custom-call | tf_op jit(solution)/shard_map/jit(cholesky)/cholesky | solution.py:99
  478.8 12.0 %cholesky.415 = f32[128,128]{1,0:T(8,128)S(1)} custom-call(f32[128,128]{1,0:T(8,128)S(1)} %convolution_subtract_fusion.9), custom_call_target="Cholesky" | custom-call | tf_op jit(solution)/shard_map/jit(cholesky)/cholesky | solution.py:99
  497.3 8.6 %while.3 = (s32[]{:T(128)}, f32[512,512]{0,1:T(8,128)S(1)}, s32[4,2]{0,1:T(2,128)S(1)}, f32[4,128,128]{2,1,0:T(8,128)S(1)}, s32[]{:T(128)}) while((s32[]{:T(128)}, f32[512,512]{0,1:T(8,128)S(1)}, s32[4,2]{0,1:T(2,128)S(1)}, f32[4,128,128]{2,1,0:T(8,128)S(1)}, s32[]{:T(128)}) %tuple.83), condition=%wide.while_cond.1, body=%wide.while_body.1.sunk | while | flops 2 | bytes 393329 | solution.py:100
  505.9 39.3 %custom-call.27 = f32[4,128,128]{1,2,0:T(8,128)S(1)} custom-call(f32[4,128,128]{2,1,0:T(8,128)S(1)} %get-tuple-element.19), custom_call_target="InvertDiagBlocksLowerTriangular" | custom-call | tf_op jit(solution)/shard_map/triangular_solve | solution.py:100
  (187 shorter events, 75.6 us)
Async XLA Ops:
  7.2 51.3 %all-gather.6.cloned.1.call-start = ((), (), s32[]{:S(2)}) async-start(), calls=%async_computation.2 | async-start | bytes 1114112 | tf_op jit(solution)/shard_map/all_gather | solution.py:53
  8.8 240.3 %all-gather.4.cloned.1.call-start = ((), (), s32[]{:S(2)}) async-start(), calls=%async_computation | async-start | bytes 4456448 | tf_op jit(solution)/shard_map/all_gather | solution.py:59
  58.5 2.4 copy-start.1
  147.2 47.8 %copy-start.4 = (f32[1,128,512]{2,1,0:T(8,128)S(1)}, f32[1,128,512]{2,1,0:T(8,128)}, u32[]{:S(2)}) copy-start(f32[1,128,512]{2,1,0:T(8,128)} %param.8) | copy-start | bytes 786436
  198.1 1.8 copy-start.5
  198.1 2.0 copy-start.6
  198.1 2.0 copy-start.7
  198.1 206.3 %all-reduce.4.cloned.1.call-start = ((), (), s32[]{:S(2)}) async-start(), calls=%async_computation.1 | async-start | bytes 2097152 | tf_op jit(solution)/shard_map/psum | solution.py:98
  254.3 20.6 %collective-permute-start = (f32[4,128,128]{2,0,1:T(4,128)S(1)}, f32[4,128,128]{2,0,1:T(4,128)S(1)}, u32[]{:S(2)}, u32[]{:S(2)}) collective-permute-start(f32[4,128,128]{2,0,1:T(4,128)S(1)} %fusion.73), channel_id=1, source_target_pairs={{0,16},{16,0},{32,48},{48,32},{64,80},{80,64},{96,112},{112,96},{1... | collective-permute-start | bytes 786440 | tf_op jit(solution)/shard_map/ppermute | solution.py:10
  257.3 27.1 %collective-permute-start.1 = (f32[4,128,128]{2,0,1:T(4,128)S(1)}, f32[4,128,128]{2,0,1:T(4,128)S(1)}, u32[]{:S(2)}, u32[]{:S(2)}) collective-permute-start(f32[4,128,128]{2,0,1:T(4,128)S(1)} %fusion.76), channel_id=1, source_target_pairs={{0,32},{16,48},{32,0},{48,16},{64,96},{80,112},{96,64},{112,80},{1... | collective-permute-start | bytes 786440 | tf_op jit(solution)/shard_map/ppermute | solution.py:10
  261.9 22.6 %collective-permute-start.2 = (f32[4,128,128]{2,0,1:T(4,128)S(1)}, f32[4,128,128]{2,0,1:T(4,128)S(1)}, u32[]{:S(2)}, u32[]{:S(2)}) collective-permute-start(f32[4,128,128]{2,0,1:T(4,128)S(1)} %fusion.79), channel_id=1, source_target_pairs={{0,64},{16,80},{32,96},{48,112},{64,0},{80,16},{96,32},{112,48},{1... | collective-permute-start | bytes 786440 | tf_op jit(solution)/shard_map/ppermute | solution.py:10
  266.7 17.7 %collective-permute-start.3 = (f32[4,128,128]{2,0,1:T(4,128)S(1)}, f32[4,128,128]{2,0,1:T(4,128)S(1)}, u32[]{:S(2)}, u32[]{:S(2)}) collective-permute-start(f32[4,128,128]{2,0,1:T(4,128)S(1)} %fusion.82), channel_id=1, source_target_pairs={{0,128},{16,144},{32,160},{48,176},{64,192},{80,208},{96,224},{112... | collective-permute-start | bytes 786440 | tf_op jit(solution)/shard_map/ppermute | solution.py:10
  270.3 14.2 %collective-permute-start.4 = (f32[4,128,128]{2,0,1:T(4,128)S(1)}, f32[4,128,128]{2,0,1:T(4,128)S(1)}, u32[]{:S(2)}, u32[]{:S(2)}) collective-permute-start(f32[4,128,128]{2,0,1:T(4,128)S(1)} %fusion.85), channel_id=1, source_target_pairs={{0,256},{16,272},{32,288},{48,304},{64,320},{80,336},{96,352},{112... | collective-permute-start | bytes 786440 | tf_op jit(solution)/shard_map/ppermute | solution.py:10
  286.7 1.0 copy-start.2
  404.4 1.7 copy-start
  406.3 1.0 copy-start.3
Sparse Core Ops, SparseCore 0:
  10.7 47.7 all-gather.5
  198.2 50.7 all-gather.3
  287.9 116.4 all-reduce.3
where the time goes:
time: 567 us; the launch traced here: 558 us
  other arithmetic  242 us (43%)
  waiting for transfers between devices  221 us (39%)
  local copies, waits for them, and re-layouts  33.7 us (6%)
  matrix products  21.9 us (4%)
  between operations  20.2 us (4%)
  starting transfers between devices  18.7 us (3%)
    psum x1, waiting for transfers between devices, per_device(): anc_pivot = lax.psum(contribution, 'front')  114 us
    another operation x15, other arithmetic, per_device(): anc_lower = jnp.linalg.cholesky(anc_pivot)  79.5 us
    another operation x14, other arithmetic, per_device(): lower = jnp.linalg.cholesky(pivot)  79 us
    all_gather x1, waiting for transfers between devices, per_device(): pivot = lax.all_gather(child_pivot[0], 'front', axis=0, tiled=True)  49.6 us
    all_gather x1, waiting for transfers between devices, per_device(): lax.all_gather(panel, 'front', axis=0, tiled=True)  47.6 us
    another operation x4, other arithmetic, per_device(): lax.linalg.triangular_solve(lower, child_panel[0], left_side=False, lower...  41.3 us
    another operation x2, other arithmetic, per_device(): lax.linalg.triangular_solve(anc_lower, assembled, left_side=False, lower=...  40.5 us
    ppermute x5, starting transfers between devices, swapped(): return lax.ppermute(value, axis, pairs)  18.6 us
  transfers between devices with their start and end apart: 8, of which 4 were waited for; matrix products, arithmetic and copies ran while one was open for 1% of the time, Pallas kernels for 0%

commit v1 on v0

--- a/solution.py
+++ b/solution.py
@@ -56,7 +56,12 @@
     panel = lax.linalg.triangular_solve(
         lower, child_panel[0], left_side=False, lower=True, transpose_a=True
     )
-    update = schur_block(panel, lax.all_gather(panel, "front", axis=0, tiled=True))
+    update = schur_block(
+        panel,
+        jnp.concatenate(
+            lax.all_to_all(jnp.stack([panel] * lax.axis_size("front")), "front", 0, 0), axis=0
+        ),
+    )
     ranks = slot_ranks(dest_list)
     slot_ids = jnp.arange(blocks_wide, dtype=jnp.int32)
     own_targets = lax.dynamic_index_in_dim(dest_list, group, 0, keepdims=False)

time: 567 us -> 621 us (1.095)
  waiting for transfers between devices: 221 us -> 263 us
    all_to_all x0 -> x1, waiting for transfers between devices: none -> 91.2 us  [per_device(): lax.all_to_all(jnp.stack([panel] * lax.axis_size('front')), 'front', 0, 0)]
    all_gather x1 -> x0, waiting for transfers between devices: 47.6 us -> none  [per_device(): lax.all_gather(panel, 'front', axis=0, tiled=True)]
    another operation x40 -> x41, local copies, waits for them, and re-layouts: 16.8 us -> 19.3 us
where the time goes in v1:
time: 621 us; the launch traced here: 611 us
  waiting for transfers between devices  263 us (42%)
  other arithmetic  242 us (39%)
  local copies, waits for them, and re-layouts  35.1 us (6%)
  matrix products  26.7 us (4%)
  starting transfers between devices  23.9 us (4%)
  between operations  20.5 us (3%)
    psum x1, waiting for transfers between devices, per_device(): anc_pivot = lax.psum(contribution, 'front')  115 us
    all_to_all x1, waiting for transfers between devices, per_device(): lax.all_to_all(jnp.stack([panel] * lax.axis_size('front')), 'front', 0, 0)  91.2 us
    another operation x15, other arithmetic, per_device(): anc_lower = jnp.linalg.cholesky(anc_pivot)  79.5 us
    another operation x14, other arithmetic, per_device(): lower = jnp.linalg.cholesky(pivot)  78.9 us
    all_gather x1, waiting for transfers between devices, per_device(): pivot = lax.all_gather(child_pivot[0], 'front', axis=0, tiled=True)  49.7 us
    another operation x4, other arithmetic, per_device(): lax.linalg.triangular_solve(lower, child_panel[0], left_side=False, lower...  40.6 us
    another operation x2, other arithmetic, per_device(): lax.linalg.triangular_solve(anc_lower, assembled, left_side=False, lower=...  40.5 us
    ppermute x5, starting transfers between devices, swapped(): return lax.ppermute(value, axis, pairs)  19.1 us
  transfers between devices with their start and end apart: 8, of which 4 were waited for; matrix products, arithmetic and copies ran while one was open for 1% of the time, Pallas kernels for 0%

profile of v1, /device:TPU:1, one launch (start us, length us, event | category | flops | bytes accessed | tf_op | source)
XLA Modules:
  0.0 611.2 jit_solution(12572366619948148588)
XLA Ops:
  8.8 49.7 %all-gather.3.cloned.1.call-done = f32[1,512,512]{2,0,1:T(1,128)} async-done(((f32[1,32,512]{2,0,1:T(1,128)}), f32[1,512,512]{2,0,1:T(1,128)}) %all-gather.3.cloned.1.call-update) | async-done | bytes 1048592 | tf_op jit(solution)/shard_map/all_gather | solution.py:53
  61.2 11.7 %cholesky.286 = f32[128,128]{1,0:T(8,128)S(1)} custom-call(f32[128,128]{1,0:T(8,128)S(1)} %cholesky.426), custom_call_target="Cholesky" | custom-call | tf_op jit(solution)/shard_map/jit(cholesky)/cholesky | solution.py:54
  73.0 9.8 %custom-call.31 = f32[1,128,128]{1,2,0:T(8,128)S(1)} custom-call(f32[1,128,128]{2,1,0:T(8,128)S(1)} %get-tuple-element.123), custom_call_target="InvertDiagBlocksLowerTriangular" | custom-call | tf_op jit(solution)/shard_map/jit(cholesky)/cholesky | solution.py:54
  83.6 11.7 %cholesky.305 = f32[128,128]{1,0:T(8,128)S(1)} custom-call(f32[128,128]{1,0:T(8,128)S(1)} %cholesky.430), custom_call_target="Cholesky" | custom-call | tf_op jit(solution)/shard_map/jit(cholesky)/cholesky | solution.py:54
  95.5 10.0 %custom-call.32 = f32[1,128,128]{1,2,0:T(8,128)S(1)} custom-call(f32[1,128,128]{2,1,0:T(8,128)S(1)} %get-tuple-element.121), custom_call_target="InvertDiagBlocksLowerTriangular" | custom-call | tf_op jit(solution)/shard_map/jit(cholesky)/cholesky | solution.py:54
  106.5 11.7 %cholesky.326 = f32[128,128]{1,0:T(8,128)S(1)} custom-call(f32[128,128]{1,0:T(8,128)S(1)} %cholesky.435), custom_call_target="Cholesky" | custom-call | tf_op jit(solution)/shard_map/jit(cholesky)/cholesky | solution.py:54
  118.4 9.8 %custom-call.33 = f32[1,128,128]{1,2,0:T(8,128)S(1)} custom-call(f32[1,128,128]{2,1,0:T(8,128)S(1)} %get-tuple-element.119), custom_call_target="InvertDiagBlocksLowerTriangular" | custom-call | tf_op jit(solution)/shard_map/jit(cholesky)/cholesky | solution.py:54
  129.0 12.1 %cholesky.343 = f32[128,128]{1,0:T(8,128)S(1)} custom-call(f32[128,128]{1,0:T(8,128)S(1)} %convolution_subtract_fusion.11), custom_call_target="Cholesky" | custom-call | tf_op jit(solution)/shard_map/jit(cholesky)/cholesky | solution.py:54
  147.1 8.5 %while.2 = (s32[]{:T(128)}, f32[512,512]{0,1:T(8,128)S(1)}, s32[4,2]{0,1:T(2,128)S(1)}, f32[4,128,128]{2,1,0:T(8,128)S(1)}, s32[]{:T(128)}) while((s32[]{:T(128)}, f32[512,512]{0,1:T(8,128)S(1)}, s32[4,2]{0,1:T(2,128)S(1)}, f32[4,128,128]{2,1,0:T(8,128)S(1)}, s32[]{:T(128)}) %tuple.71), condition=%wide.while_cond, body=%wide.while_body.sunk | while | flops 2 | bytes 393329 | solution.py:56
  155.6 39.3 %custom-call.26 = f32[4,128,128]{1,2,0:T(8,128)S(1)} custom-call(f32[4,128,128]{2,1,0:T(8,128)S(1)} %get-tuple-element.11), custom_call_target="InvertDiagBlocksLowerTriangular" | custom-call | tf_op jit(solution)/shard_map/triangular_solve | solution.py:56
  200.0 4.7 all-to-all-start
  207.0 91.2 %all-to-all-done = f32[16,128,512]{2,1,0:T(8,128)} async-done(((f32[16,128,512]{2,1,0:T(8,128)}), f32[16,128,512]{2,1,0:T(8,128)}, u32[]{:S(2)}, u32[]{:S(2)}) %all-to-all-start) | async-done | bytes 4194336 | tf_op jit(solution)/shard_map/all_to_all | solution.py:62
  298.2 6.3 %fusion.29 = f32[128,16,128]{2,0,1:T(8,128)S(1)} fusion(f32[16,128,512]{2,1,0:T(8,128)} %all-to-all-done, f32[128,128]{0,1:T(8,128)S(1)} %fusion.59, f32[128,128]{0,1:T(8,128)S(1)} %fusion.60, f32[128,128]{0,1:T(8,128)S(1)} %fusion.61, f32[128,128]{0,1:T(8,128)S(1)} %bitcast.161), kind=kOutput, calls=%fused_computation.64 | convolution fusion | flops 1610809344 | bytes 5505024 | tf_op jit(solution)/shard_map/dot_general | solution.py:14
  329.2 7.3 %collective-permute-done.1 = f32[4,128,128]{2,0,1:T(4,128)S(1)} collective-permute-done((f32[4,128,128]{2,0,1:T(4,128)S(1)}, f32[4,128,128]{2,0,1:T(4,128)S(1)}, u32[]{:S(2)}, u32[]{:S(2)}) %collective-permute-start.1) | collective-permute-done | bytes 262176 | tf_op jit(solution)/shard_map/ppermute | solution.py:10
  342.6 114.9 %all-reduce.4.cloned.1.call-done = f32[512,512]{0,1:T(8,128)} async-done(((f32[512,512]{0,1:T(8,128)}), f32[512,512]{0,1:T(8,128)}) %all-reduce.4.cloned.1.call-update) | async-done | bytes 1048592 | tf_op jit(solution)/shard_map/psum | solution.py:103
  460.3 11.7 %cholesky.358 = f32[128,128]{1,0:T(8,128)S(1)} custom-call(f32[128,128]{1,0:T(8,128)S(1)} %cholesky.439), custom_call_target="Cholesky" | custom-call | tf_op jit(solution)/shard_map/jit(cholesky)/cholesky | solution.py:104
  472.2 9.8 %custom-call.34 = f32[1,128,128]{1,2,0:T(8,128)S(1)} custom-call(f32[1,128,128]{2,1,0:T(8,128)S(1)} %get-tuple-element.117), custom_call_target="InvertDiagBlocksLowerTriangular" | custom-call | tf_op jit(solution)/shard_map/jit(cholesky)/cholesky | solution.py:104
  484.6 11.9 %cholesky.377 = f32[128,128]{1,0:T(8,128)S(1)} custom-call(f32[128,128]{1,0:T(8,128)S(1)} %cholesky.443), custom_call_target="Cholesky" | custom-call | tf_op jit(solution)/shard_map/jit(cholesky)/cholesky | solution.py:104
  496.7 9.8 %custom-call.35 = f32[1,128,128]{1,2,0:T(8,128)S(1)} custom-call(f32[1,128,128]{2,1,0:T(8,128)S(1)} %get-tuple-element.115), custom_call_target="InvertDiagBlocksLowerTriangular" | custom-call | tf_op jit(solution)/shard_map/jit(cholesky)/cholesky | solution.py:104
  508.5 11.7 %cholesky.398 = f32[128,128]{1,0:T(8,128)S(1)} custom-call(f32[128,128]{1,0:T(8,128)S(1)} %cholesky.448), custom_call_target="Cholesky" | custom-call | tf_op jit(solution)/shard_map/jit(cholesky)/cholesky | solution.py:104
  520.4 9.8 %custom-call.36 = f32[1,128,128]{1,2,0:T(8,128)S(1)} custom-call(f32[1,128,128]{2,1,0:T(8,128)S(1)} %get-tuple-element.113), custom_call_target="InvertDiagBlocksLowerTriangular" | custom-call | tf_op jit(solution)/shard_map/jit(cholesky)/cholesky | solution.py:104
  531.8 12.0 %cholesky.415 = f32[128,128]{1,0:T(8,128)S(1)} custom-call(f32[128,128]{1,0:T(8,128)S(1)} %convolution_subtract_fusion.9), custom_call_target="Cholesky" | custom-call | tf_op jit(solution)/shard_map/jit(cholesky)/cholesky | solution.py:104
  550.3 8.6 %while.3 = (s32[]{:T(128)}, f32[512,512]{0,1:T(8,128)S(1)}, s32[4,2]{0,1:T(2,128)S(1)}, f32[4,128,128]{2,1,0:T(8,128)S(1)}, s32[]{:T(128)}) while((s32[]{:T(128)}, f32[512,512]{0,1:T(8,128)S(1)}, s32[4,2]{0,1:T(2,128)S(1)}, f32[4,128,128]{2,1,0:T(8,128)S(1)}, s32[]{:T(128)}) %tuple.81), condition=%wide.while_cond.1, body=%wide.while_body.1.sunk | while | flops 2 | bytes 393329 | solution.py:105
  559.0 39.3 %custom-call.27 = f32[4,128,128]{1,2,0:T(8,128)S(1)} custom-call(f32[4,128,128]{2,1,0:T(8,128)S(1)} %get-tuple-element.19), custom_call_target="InvertDiagBlocksLowerTriangular" | custom-call | tf_op jit(solution)/shard_map/triangular_solve | solution.py:105
  (189 shorter events, 84.2 us)
Async XLA Ops:
  7.2 51.3 %all-gather.3.cloned.1.call-start = ((), (), s32[]{:S(2)}) async-start(), calls=%async_computation.2 | async-start | bytes 1114112 | tf_op jit(solution)/shard_map/all_gather | solution.py:53
  58.5 2.4 copy-start.1
  147.1 47.8 %copy-start.5 = (f32[1,128,512]{2,1,0:T(8,128)S(1)}, f32[1,128,512]{2,1,0:T(8,128)}, u32[]{:S(2)}) copy-start(f32[1,128,512]{2,1,0:T(8,128)} %param.8) | copy-start | bytes 786436
  200.0 4.8 copy-start.4
  200.0 98.2 %all-to-all-start = ((f32[16,128,512]{2,1,0:T(8,128)}), f32[16,128,512]{2,1,0:T(8,128)}, u32[]{:S(2)}, u32[]{:S(2)}) async-start(f32[16,128,512]{2,1,0:T(8,128)} %stack.26), calls=%async_computation | async-start | bytes 8388608 | tf_op jit(solution)/shard_map/all_to_all | solution.py:62
  204.7 0.7 copy-start.6
  204.7 0.9 copy-start.7
  204.7 0.9 copy-start.8
  204.7 252.7 %all-reduce.4.cloned.1.call-start = ((), (), s32[]{:S(2)}) async-start(), calls=%async_computation.1 | async-start | bytes 2097152 | tf_op jit(solution)/shard_map/psum | solution.py:103
  305.6 23.5 %collective-permute-start = (f32[4,128,128]{2,0,1:T(4,128)S(1)}, f32[4,128,128]{2,0,1:T(4,128)S(1)}, u32[]{:S(2)}, u32[]{:S(2)}) collective-permute-start(f32[4,128,128]{2,0,1:T(4,128)S(1)} %fusion.14), channel_id=1, source_target_pairs={{0,16},{16,0},{32,48},{48,32},{64,80},{80,64},{96,112},{112,96},{1... | collective-permute-start | bytes 786440 | tf_op jit(solution)/shard_map/ppermute | solution.py:10
  309.8 26.7 %collective-permute-start.1 = (f32[4,128,128]{2,0,1:T(4,128)S(1)}, f32[4,128,128]{2,0,1:T(4,128)S(1)}, u32[]{:S(2)}, u32[]{:S(2)}) collective-permute-start(f32[4,128,128]{2,0,1:T(4,128)S(1)} %fusion.12), channel_id=1, source_target_pairs={{0,32},{16,48},{32,0},{48,16},{64,96},{80,112},{96,64},{112,80},{1... | collective-permute-start | bytes 786440 | tf_op jit(solution)/shard_map/ppermute | solution.py:10
  314.9 21.6 %collective-permute-start.2 = (f32[4,128,128]{2,0,1:T(4,128)S(1)}, f32[4,128,128]{2,0,1:T(4,128)S(1)}, u32[]{:S(2)}, u32[]{:S(2)}) collective-permute-start(f32[4,128,128]{2,0,1:T(4,128)S(1)} %fusion.10), channel_id=1, source_target_pairs={{0,64},{16,80},{32,96},{48,112},{64,0},{80,16},{96,32},{112,48},{1... | collective-permute-start | bytes 786440 | tf_op jit(solution)/shard_map/ppermute | solution.py:10
  320.4 16.1 %collective-permute-start.3 = (f32[4,128,128]{2,0,1:T(4,128)S(1)}, f32[4,128,128]{2,0,1:T(4,128)S(1)}, u32[]{:S(2)}, u32[]{:S(2)}) collective-permute-start(f32[4,128,128]{2,0,1:T(4,128)S(1)} %fusion.8), channel_id=1, source_target_pairs={{0,128},{16,144},{32,160},{48,176},{64,192},{80,208},{96,224},{112... | collective-permute-start | bytes 786440 | tf_op jit(solution)/shard_map/ppermute | solution.py:10
  324.6 12.0 %collective-permute-start.4 = (f32[4,128,128]{2,0,1:T(4,128)S(1)}, f32[4,128,128]{2,0,1:T(4,128)S(1)}, u32[]{:S(2)}, u32[]{:S(2)}) collective-permute-start(f32[4,128,128]{2,0,1:T(4,128)S(1)} %fusion.6), channel_id=1, source_target_pairs={{0,256},{16,272},{32,288},{48,304},{64,320},{80,336},{96,352},{112... | collective-permute-start | bytes 786440 | tf_op jit(solution)/shard_map/ppermute | solution.py:10
  338.8 1.0 copy-start.2
  457.4 1.7 copy-start
  459.3 1.0 copy-start.3
Sparse Core Ops, SparseCore 0:
  10.7 47.7 all-gather.2
  340.0 117.4 all-reduce.3
